TPU v7x, 512 devices: a whole 4x8x8 slice. The times are simulated.
512 devices in a mesh: row: 16 (over x, y_hi), col: 32 (over z, y_lo, core).
Axes of the slice: x: 4, y: 8 (y_hi: 4, y_lo: 2; y = y_hi * 2 + y_lo), z: 8, core: 2. Of those that a mesh axis runs over, the one named last changes fastest.
Arguments:
- left_factor: float32 [8192, 512], P(('row', 'col')), may hold values from -0.0625 to 0.0625
- left_cotangent: float32 [8192, 512], P(('row', 'col')), may hold values from -80 to 80
- right_factor: float32 [24576, 512], P(('col', 'row')), may hold values from -0.0390625 to 0.0390625
- right_cotangent: float32 [24576, 512], P(('col', 'row')), may hold values from -80 to 80
- singular: float32 [512], replicated, may hold values from 0.5 to 2, as said below
- singular_cotangent: float32 [512], replicated, may hold values from -384 to 384
Outputs:
- matrix_cotangent: float32 [8192, 24576], P('row', 'col')
Inputs may be any that keep to these rules, and one draw needn't show every extreme that they name: `singular`: strictly decreasing; consecutive values differ by at least 0.75 / 512.
All inputs are finite; a program needn't handle non-finite values.
Results may differ from a plain program's by a relative error of at most 0.0003.
Values sent between devices are 32-bit elements; how exact they have to be, the bound alone decides.
No kernel may reach another device: no remote copies, remote signals or barrier semaphores. Data moves between devices by JAX's collectives and lax.ppermute only.
A program may use at most 64 MiB of HBM per device.

v0:
```python
import jax
import jax.numpy as jnp
from jax import lax
from jax.experimental import pallas as pl
from jax.experimental.pallas import tpu as pltpu
from jax.sharding import Mesh
from jax.sharding import PartitionSpec as P

ROW = ("x", "yh")
COL = ("zh", "zl", "yl", "core")
ALL = ROW + COL
Z = ("zh", "zl")
OUTER = ("x", "zl", "yl")
INNER = ("yh", "zh")
SIZES = (4, 4, 4, 2, 2, 2)
SIZE_K = 512
HALF = 256
PRODUCT_LIMIT = 50 << 20
HIGHEST = lax.Precision.HIGHEST
SWAP = [(0, 1), (1, 0)]


def dot(a, b, contract, precision):
    return lax.dot_general(
        a, b, (contract, ((), ())), precision=precision, preferred_element_type=jnp.float32
    )


def gather(block, axis, size):
    copies = jnp.broadcast_to(block[None], (size,) + block.shape)
    return lax.all_to_all(copies, axis, 0, 0)


def shift(block, axis, size, by):
    return lax.ppermute(block, axis, [(i, (i + by) % size) for i in range(size)])


def swap(block):
    return lax.ppermute(block, "core", SWAP)


def pack_kernel(left, left_cot, right, right_cot, right_pair, left_pair, stacked, held, sems):
    low, high = pl.ds(0, SIZE_K), pl.ds(SIZE_K, SIZE_K)
    top, bottom = pl.ds(0, 48), pl.ds(48, 16)

    def start(i, source, target):
        copy = pltpu.make_async_copy(source, target, sems.at[i])
        copy.start()
        return copy

    reads = [
        start(0, right_cot, held.at[top, low]),
        start(1, right, held.at[top, high]),
        start(2, left, held.at[bottom, low]),
        start(3, left_cot, held.at[bottom, high]),
    ]
    for copy in reads:
        copy.wait()
    writes = [
        start(4, held, stacked),
        start(5, held.at[top, :], right_pair),
        start(6, held.at[bottom, :], left_pair),
    ]
    for copy in writes:
        copy.wait()


def pack(left, left_cot, right, right_cot):
    shapes = ((48, 1024), (16, 1024), (64, 1024))
    hbm = pl.BlockSpec(memory_space=pl.ANY)
    return pl.pallas_call(
        pack_kernel,
        out_shape=[jax.ShapeDtypeStruct(s, jnp.float32) for s in shapes],
        in_specs=[hbm] * 4,
        out_specs=[hbm] * 3,
        scratch_shapes=[
            pltpu.VMEM((64, 1024), jnp.float32),
            pltpu.SemaphoreType.DMA((7,)),
        ],
        cost_estimate=pl.CostEstimate(flops=0, bytes_accessed=1 << 20, transcendentals=0),
        name="pack",
    )(left, left_cot, right, right_cot)


def half_core_kernel(core_index, own, got, s_row, out, lhs, rhs, lhs2, rhs2):
    begin = pl.multiple_of(core_index[0] * HALF, HALF)
    half = pl.ds(begin, HALF)
    cot_half = pl.ds(pl.multiple_of(begin + SIZE_K, HALF), HALF)
    s_all = s_row[...]
    s_half = s_row[:, half]
    inv_all = 1.0 / s_all
    inv_half = 1.0 / s_half
    for i, block in enumerate((own, got)):
        left = pl.ds(16 * i, 16)
        lhs[left, :] = block[48:, half]
        rhs[left, :] = block[48:, SIZE_K:] * s_all
        lhs2[left, :] = block[48:, half]
        rhs2[left, :] = block[48:, SIZE_K:] * inv_all
        left = pl.ds(32 + 16 * i, 16)
        lhs[left, :] = -block[48:, cot_half]
        rhs[left, :] = block[48:, :SIZE_K] * s_all
        right = pl.ds(64 + 48 * i, 48)
        lhs[right, :] = block[:48, cot_half] * s_half
        rhs[right, :] = block[:48, :SIZE_K]
        right = pl.ds(160 + 48 * i, 48)
        lhs[right, :] = -block[:48, half] * s_half
        rhs[right, :] = block[:48, SIZE_K:]
        right = pl.ds(32 + 48 * i, 48)
        lhs2[right, :] = block[:48, half] * inv_half
        rhs2[right, :] = block[:48, SIZE_K:]
    rows = ((0,), (0,))
    eye = lax.broadcasted_iota(jnp.int32, (HALF, HALF), 0) == (
        lax.broadcasted_iota(jnp.int32, (HALF, HALF), 1)
    )
    s_down = jnp.sum(jnp.where(eye, s_half, 0.0), axis=1, keepdims=True)
    spread = s_all * s_all - s_down * s_down
    diagonal = (lax.broadcasted_iota(jnp.int32, (HALF, SIZE_K), 0) + begin) == (
        lax.broadcasted_iota(jnp.int32, (HALF, SIZE_K), 1)
    )
    divided = jnp.where(diagonal, 0.0, 1.0 / jnp.where(diagonal, 1.0, spread))
    main = dot(lhs[...], rhs[...], rows, HIGHEST)
    out[...] = divided * main - dot(lhs2[...], rhs2[...], rows, HIGHEST)


def half_core(core_index, own, got, singular):
    vmem = pl.BlockSpec(memory_space=pltpu.VMEM)
    return pl.pallas_call(
        half_core_kernel,
        out_shape=jax.ShapeDtypeStruct((HALF, SIZE_K), jnp.float32),
        in_specs=[pl.BlockSpec(memory_space=pltpu.SMEM)] + [vmem] * 3,
        out_specs=vmem,
        scratch_shapes=[
            pltpu.VMEM((256, HALF), jnp.float32),
            pltpu.VMEM((256, SIZE_K), jnp.float32),
            pltpu.VMEM((128, HALF), jnp.float32),
            pltpu.VMEM((128, SIZE_K), jnp.float32),
        ],
        cost_estimate=pl.CostEstimate(
            flops=2 * 6 * 384 * HALF * SIZE_K, bytes_accessed=1 << 20, transcendentals=0
        ),
        compiler_params=pltpu.CompilerParams(vmem_limit_bytes=12 << 20),
        name="half_core",
    )(core_index.reshape(1), own, got, singular.reshape(1, -1))


def place_kernel(z, below, own, above, mid_below, mid_above, last_above, out):
    blocks = [own[...], above[...], mid_above[0], mid_above[1], last_above[...]]
    blocks = blocks + [mid_below[0], mid_below[1], below[...]]
    for i, block in enumerate(blocks):
        out[lax.rem(z[0] + i, 8)] = block


def merge_kernel(index, mine, theirs, out):
    out[:, index[0]] = mine[...]
    out[:, 1 - index[0]] = theirs[...]


def assemble(kernel, shape, index, *blocks):
    vmem = pl.BlockSpec(memory_space=pltpu.VMEM)
    return pl.pallas_call(
        kernel,
        out_shape=jax.ShapeDtypeStruct(shape, jnp.float32),
        in_specs=[pl.BlockSpec(memory_space=pltpu.SMEM)] + [vmem] * len(blocks),
        out_specs=vmem,
        cost_estimate=pl.CostEstimate(flops=0, bytes_accessed=2 << 20, transcendentals=0),
        compiler_params=pltpu.CompilerParams(vmem_limit_bytes=10 << 20),
    )(index.reshape(1), *blocks)


def split(a):
    high = a.astype(jnp.bfloat16)
    return high, (a - high.astype(jnp.float32)).astype(jnp.bfloat16)


def dot3(a, b, contract):
    a_high, a_low = a
    b_high, b_low = b
    small = dot(a_high, b_low, contract, None) + dot(a_low, b_high, contract, None)
    return dot(a_high, b_high, contract, None) + small


def panel_kernel(core_index, lefts, own_half, other_half, s_row, cot_row, high, low, core):
    first = pl.ds(pl.multiple_of(core_index[0] * HALF, HALF), HALF)
    second = pl.ds(pl.multiple_of((1 - core_index[0]) * HALF, HALF), HALF)
    core[first, :] = own_half[...]
    core[second, :] = other_half[...]
    inverse = 1.0 / s_row[...]
    factor = lefts[:, :SIZE_K]
    high[:, :SIZE_K], low[:, :SIZE_K] = split(factor * inverse)
    whole = dot3(split(factor), split(core[...]), ((1,), (0,)))
    whole = whole + factor * cot_row[...] + lefts[:, SIZE_K:] * inverse
    high[:, SIZE_K:], low[:, SIZE_K:] = split(whole)


def panel(core_index, lefts, own_half, other_half, singular, singular_cot):
    vmem = pl.BlockSpec(memory_space=pltpu.VMEM)
    return pl.pallas_call(
        panel_kernel,
        out_shape=[jax.ShapeDtypeStruct((512, 2 * SIZE_K), jnp.bfloat16)] * 2,
        in_specs=[pl.BlockSpec(memory_space=pltpu.SMEM)] + [vmem] * 5,
        out_specs=[vmem] * 2,
        scratch_shapes=[pltpu.VMEM((SIZE_K, SIZE_K), jnp.float32)],
        cost_estimate=pl.CostEstimate(
            flops=6 * 512 * SIZE_K * SIZE_K, bytes_accessed=5 << 20, transcendentals=0
        ),
        compiler_params=pltpu.CompilerParams(vmem_limit_bytes=24 << 20),
        name="panel",
    )(
        core_index.reshape(1),
        lefts,
        own_half,
        other_half,
        singular.reshape(1, -1),
        singular_cot.reshape(1, -1),
    )


def product_kernel(high, low, rights, out):
    out[...] = dot3((high[...], low[...]), split(rights[...]), ((1,), (1,)))


def product(high, low, rights):
    width = 2 * SIZE_K
    step = 256
    whole = pl.BlockSpec((512, width), lambda i: (0, 0))
    return pl.pallas_call(
        product_kernel,
        out_shape=jax.ShapeDtypeStruct((512, 768), jnp.float32),
        grid=(768 // step,),
        in_specs=[whole, whole, pl.BlockSpec((step, width), lambda i: (i, 0))],
        out_specs=pl.BlockSpec((512, step), lambda i: (0, i)),
        cost_estimate=pl.CostEstimate(
            flops=6 * 512 * 768 * width, bytes_accessed=7 << 20, transcendentals=0
        ),
        compiler_params=pltpu.CompilerParams(vmem_limit_bytes=PRODUCT_LIMIT),
        name="product",
    )(high, low, rights)


def local(left, left_cot, right, right_cot, singular, singular_cot):
    core_index = lax.axis_index("core")
    at_low = lax.axis_index("yl") == 0

    right_pair, left_pair, stacked = pack(left, left_cot, right, right_cot)
    rights = lax.all_gather(right_pair, ROW, axis=0, tiled=True)
    other = shift(left_pair, "yl", 2, 1)
    got = swap(stacked)
    mine = half_core(core_index, stacked, got, singular)
    pieces = lax.all_to_all(mine.reshape(16, 16, SIZE_K), OUTER, 0, 0)

    own = jnp.stack([jnp.where(at_low, left_pair, other), jnp.where(at_low, other, left_pair)])
    below, above = shift(own, Z, 8, 1), shift(own, Z, 8, -1)

    mid_below = shift(jnp.stack([below, own]), Z, 8, 2)
    mid_above = shift(jnp.stack([own, above]), Z, 8, -2)
    pieces = gather(jnp.sum(pieces, axis=0), INNER, 16)
    last_above = shift(mid_above[1], Z, 8, -1)
    blocks = (below, own, above, mid_below, mid_above, last_above)
    line = assemble(place_kernel, (8, 2, 16, 1024), lax.axis_index(Z), *blocks)
    line = line.reshape(16, 16, 1024)
    rows = jnp.sum(pieces, axis=0)
    own_half = gather(rows, OUTER, 16).reshape(HALF, SIZE_K)
    other_line = swap(line)
    lefts = assemble(
        merge_kernel, (16, 2, 16, 1024), core_index, line, other_line
    ).reshape(-1, 1024)
    other_half = swap(own_half)
    high, low = panel(core_index, lefts, own_half, other_half, singular, singular_cot)
    return product(high, low, rights)


def solution(mesh):
    fine = Mesh(mesh.devices.reshape(SIZES), ALL)
    placed = (
        P(ROW + COL, None),
        P(ROW + COL, None),
        P(COL + ROW, None),
        P(COL + ROW, None),
        P(),
        P(),
    )
    return jax.shard_map(local, mesh=fine, in_specs=placed, out_specs=P(ROW, COL), check_vma=False)
```

profile of v0, /device:TPU:1, one launch (start us, length us, event | category | flops | bytes accessed | tf_op | source)
XLA Modules:
  0.0 123.4 jit_solution(5857754572861204354)
XLA Ops:
  6.5 1.8 %pack.1 = (f32[48,1024]{1,0:T(8,128)}, f32[16,1024]{1,0:T(8,128)}, f32[64,1024]{1,0:T(8,128)}) custom-call(f32[16,512]{1,0:T(8,128)} %left.1, f32[16,512]{1,0:T(8,128)} %left_cot.1, f32[48,512]{1,0:T(8,128)} %right.1, f32[48,512]{1,0:T(8,128)} %right_cot.1), custom_call_target="tpu_custom_call" | custom-call | bytes 1048576 | tf_op jit(solution)/shard_map/pack/pallas_call | solution.py:71
  8.3 0.0 all-gather.2.cloned.1.call-update
  8.3 8.7 %collective-permute-start.7 = (f32[64,1024]{1,0:T(8,128)}, f32[64,1024]{1,0:T(8,128)S(1)}, u32[]{:S(2)}, u32[]{:S(2)}) collective-permute-start(f32[64,1024]{1,0:T(8,128)} %get-tuple-element.11.own), channel_id=1, source_target_pairs={{0,1},{1,0},{2,3},{3,2},{4,5},{5,4},{6,7},{7,6},{8,9},{9,8},{10,11... | collective-permute-start | bytes 786440 | tf_op jit(solution)/shard_map/ppermute | solution.py:39
  17.1 1.3 %collective-permute-done.7.got = f32[64,1024]{1,0:T(8,128)S(1)} collective-permute-done((f32[64,1024]{1,0:T(8,128)}, f32[64,1024]{1,0:T(8,128)S(1)}, u32[]{:S(2)}, u32[]{:S(2)}) %collective-permute-start.7) | collective-permute-done | bytes 262176 | tf_op jit(solution)/shard_map/ppermute | solution.py:39
  18.5 0.7 copy-done
  19.1 0.9 copy-done.3
  20.1 1.1 half_core.1
  21.2 11.0 %all_to_all.15 = f32[16,16,512]{2,1,0:T(8,128)S(1)} all-to-all(f32[16,16,512]{2,1,0:T(8,128)S(1)} %bitcast.25), channel_id=1, replica_groups=mesh['x'=4,'yh'=4,'zh'=4,'zl'=2,'yl'=2,'core'=2] {'x','zl','yl'}, dimensions={0} | all-to-all | bytes 1048576 | tf_op jit(solution)/shard_map/all_to_all | solution.py:249
  32.2 0.9 broadcast_in_dim.4
  33.1 12.4 %all-to-all-start.1 = ((f32[16,16,512]{2,1,0:T(8,128)}), f32[16,16,512]{2,1,0:T(8,128)S(1)}, u32[]{:S(2)}, u32[]{:S(2)}) async-start(f32[16,16,512]{2,1,0:T(8,128)} %broadcast_in_dim.4), calls=%async_computation.1 | async-start | bytes 1048576 | tf_op jit(solution)/shard_map/all_to_all | solution.py:31
  45.5 3.7 %collective-permute-start = (f32[16,1024]{1,0:T(8,128)S(1)}, f32[16,1024]{1,0:T(8,128)S(1)}, u32[]{:S(2)}, u32[]{:S(2)}) collective-permute-start(f32[16,1024]{1,0:T(8,128)S(1)} %copy-done.4), channel_id=1, source_target_pairs={{0,2},{2,0},{1,3},{3,1},{4,6},{6,4},{5,7},{7,5},{8,10},{10,8},{9,1... | collective-permute-start | bytes 196616 | tf_op jit(solution)/shard_map/ppermute | solution.py:35
  49.2 11.0 %collective-permute-done = f32[16,1024]{1,0:T(8,128)S(1)} collective-permute-done((f32[16,1024]{1,0:T(8,128)S(1)}, f32[16,1024]{1,0:T(8,128)S(1)}, u32[]{:S(2)}, u32[]{:S(2)}) %collective-permute-start) | collective-permute-done | bytes 65568 | tf_op jit(solution)/shard_map/ppermute | solution.py:35
  60.2 5.6 %collective-permute-start.1 = (f32[2,16,1024]{2,1,0:T(8,128)S(1)}, f32[2,16,1024]{2,1,0:T(8,128)S(1)}, u32[]{:S(2)}, u32[]{:S(2)}) collective-permute-start(f32[2,16,1024]{2,1,0:T(8,128)S(1)} %get-tuple-element.18.own), channel_id=1, source_target_pairs={{0,4},{4,8},{8,12},{12,16},{16,20},{20,24},{24,28},{28,0},{1,5},{5... | collective-permute-start | bytes 393224 | tf_op jit(solution)/shard_map/ppermute | solution.py:35
  65.8 4.0 %collective-permute-start.2 = (f32[2,16,1024]{2,1,0:T(8,128)S(1)}, f32[2,16,1024]{2,1,0:T(8,128)S(1)}, u32[]{:S(2)}, u32[]{:S(2)}) collective-permute-start(f32[2,16,1024]{2,1,0:T(8,128)S(1)} %get-tuple-element.18.own), channel_id=1, source_target_pairs={{0,28},{4,0},{8,4},{12,8},{16,12},{20,16},{24,20},{28,24},{1,29},{... | collective-permute-start | bytes 393224 | tf_op jit(solution)/shard_map/ppermute | solution.py:35
  69.8 0.8 collective-permute-done.1.below
  70.6 1.3 %collective-permute-done.2.above = f32[2,16,1024]{2,1,0:T(8,128)S(1)} collective-permute-done((f32[2,16,1024]{2,1,0:T(8,128)S(1)}, f32[2,16,1024]{2,1,0:T(8,128)S(1)}, u32[]{:S(2)}, u32[]{:S(2)}) %collective-permute-start.2) | collective-permute-done | bytes 131104 | tf_op jit(solution)/shard_map/ppermute | solution.py:35
  72.0 5.1 %collective-permute-start.4 = (f32[2,2,16,1024]{3,2,1,0:T(8,128)S(1)}, f32[2,2,16,1024]{3,2,1,0:T(8,128)S(1)}, u32[]{:S(2)}, u32[]{:S(2)}) collective-permute-start(f32[2,2,16,1024]{3,2,1,0:T(8,128)S(1)} %get-tuple-element.15), channel_id=1, source_target_pairs={{0,24},{4,28},{8,0},{12,4},{16,8},{20,12},{24,16},{28,20},{1,25},{... | collective-permute-start | bytes 786440 | tf_op jit(solution)/shard_map/ppermute | solution.py:35
  77.2 0.9 broadcast_in_dim.5
  78.0 3.6 %all-to-all-start.2 = ((f32[16,16,512]{2,1,0:T(8,128)}), f32[16,16,512]{2,1,0:T(8,128)S(1)}, u32[]{:S(2)}, u32[]{:S(2)}) async-start(f32[16,16,512]{2,1,0:T(8,128)} %broadcast_in_dim.5), calls=%async_computation.2 | async-start | bytes 1048576 | tf_op jit(solution)/shard_map/all_to_all | solution.py:31
  81.6 1.9 %collective-permute-start.3 = (f32[2,2,16,1024]{3,2,1,0:T(8,128)S(1)}, f32[2,2,16,1024]{3,2,1,0:T(8,128)S(1)}, u32[]{:S(2)}, u32[]{:S(2)}) collective-permute-start(f32[2,2,16,1024]{3,2,1,0:T(8,128)S(1)} %get-tuple-element.16), channel_id=1, source_target_pairs={{0,8},{4,12},{8,16},{12,20},{16,24},{20,28},{24,0},{28,4},{1,9},{5... | collective-permute-start | bytes 786440 | tf_op jit(solution)/shard_map/ppermute | solution.py:35
  83.5 0.5 collective-permute-done.4.mid_above
  84.1 8.9 %collective-permute-start.5 = (f32[2,16,1024]{2,1,0:T(8,128)S(1)}, f32[2,16,1024]{2,1,0:T(8,128)S(1)}, u32[]{:S(2)}, u32[]{:S(2)}) collective-permute-start(f32[2,16,1024]{2,1,0:T(8,128)S(1)} %slice_bitcast_fusion), channel_id=1, source_target_pairs={{0,28},{4,0},{8,4},{12,8},{16,12},{20,16},{24,20},{28,24},{1,29},{... | collective-permute-start | bytes 393224 | tf_op jit(solution)/shard_map/ppermute | solution.py:35
  93.0 9.0 %collective-permute-done.3.mid_below = f32[2,2,16,1024]{3,2,1,0:T(8,128)S(1)} collective-permute-done((f32[2,2,16,1024]{3,2,1,0:T(8,128)S(1)}, f32[2,2,16,1024]{3,2,1,0:T(8,128)S(1)}, u32[]{:S(2)}, u32[]{:S(2)}) %collective-permute-start.3) | collective-permute-done | bytes 262176 | tf_op jit(solution)/shard_map/ppermute | solution.py:35
  102.0 0.1 shard_map.64
  102.1 3.8 %collective-permute-start.6 = (f32[16,16,1024]{2,1,0:T(8,128)S(1)}, f32[16,16,1024]{2,1,0:T(8,128)S(1)}, u32[]{:S(2)}, u32[]{:S(2)}) collective-permute-start(f32[16,16,1024]{2,1,0:T(8,128)S(1)} %bitcast.19), channel_id=1, source_target_pairs={{0,1},{1,0},{2,3},{3,2},{4,5},{5,4},{6,7},{7,6},{8,9},{9,8},{10,11... | collective-permute-start | bytes 3145736 | tf_op jit(solution)/shard_map/ppermute | solution.py:39
  106.0 1.9 %collective-permute-start.8 = (f32[256,512]{1,0:T(8,128)S(1)}, f32[256,512]{1,0:T(8,128)S(1)}, u32[]{:S(2)}, u32[]{:S(2)}) collective-permute-start(f32[256,512]{1,0:T(8,128)S(1)} %bitcast.21), channel_id=1, source_target_pairs={{0,1},{1,0},{2,3},{3,2},{4,5},{5,4},{6,7},{7,6},{8,9},{9,8},{10,11... | collective-permute-start | bytes 1572872 | tf_op jit(solution)/shard_map/ppermute | solution.py:39
  107.9 0.3 collective-permute-done.6.theirs
  108.2 0.1 shard_map.65
  108.3 1.4 %collective-permute-done.8.other_half = f32[256,512]{1,0:T(8,128)S(1)} collective-permute-done((f32[256,512]{1,0:T(8,128)S(1)}, f32[256,512]{1,0:T(8,128)S(1)}, u32[]{:S(2)}, u32[]{:S(2)}) %collective-permute-start.8) | collective-permute-done | bytes 524320 | tf_op jit(solution)/shard_map/ppermute | solution.py:39
  109.8 1.3 %panel.1 = (bf16[512,1024]{1,0:T(8,128)(2,1)S(1)}, bf16[512,1024]{1,0:T(8,128)(2,1)S(1)}) custom-call(s32[1]{0:T(128)} %bitcast.index.core_index, f32[512,1024]{1,0:T(8,128)S(1)} %bitcast.18, f32[256,512]{1,0:T(8,128)S(1)} %bitcast.22, f32[256,512]{1,0:T(8,128)S(1)} %collective-permute-done.8.other_half, f32[1,512]{1,0:T(1,128)S(1)} %bitcast.27, ...), custom_call_target="tpu_custom_call" | custom-call | flops 805306368 | bytes 5242880 | tf_op jit(solution)/shard_map/panel/pallas_call | solution.py:197
  111.0 0.0 all-gather.2.cloned.1.call-done.rights
  111.1 5.5 %product.1 = f32[512,768]{1,0:T(8,128)} custom-call(bf16[512,1024]{1,0:T(8,128)(2,1)S(1)} %get-tuple-element.12.high, bf16[512,1024]{1,0:T(8,128)(2,1)S(1)} %get-tuple-element.13.low, f32[768,1024]{1,0:T(8,128)} %all-gather.2.cloned.1.call-done.rights), custom_call_target="tpu_custom_call" | custom-call | flops 2415919104 | bytes 7340032 | tf_op jit(solution)/shard_map/product/pallas_call | solution.py:226
  (18 shorter events, 0.2 us)
Async XLA Ops:
  6.5 104.5 %all-gather.2.cloned.1.call-start = ((), (), s32[]{:S(2)}) async-start(), calls=%async_computation.3 | async-start | bytes 3342336 | tf_op jit(solution)/shard_map/all_gather | solution.py:245
  8.3 10.1 %collective-permute-start.7 = (f32[64,1024]{1,0:T(8,128)}, f32[64,1024]{1,0:T(8,128)S(1)}, u32[]{:S(2)}, u32[]{:S(2)}) collective-permute-start(f32[64,1024]{1,0:T(8,128)} %get-tuple-element.11.own), channel_id=1, source_target_pairs={{0,1},{1,0},{2,3},{3,2},{4,5},{5,4},{6,7},{7,6},{8,9},{9,8},{10,11... | collective-permute-start | bytes 786440 | tf_op jit(solution)/shard_map/ppermute | solution.py:39
  18.5 0.7 copy-start
  19.1 0.9 copy-start.3
  21.2 24.2 %copy-start.4 = (f32[16,1024]{1,0:T(8,128)S(1)}, f32[16,1024]{1,0:T(8,128)}, u32[]{:S(2)}) copy-start(f32[16,1024]{1,0:T(8,128)} %get-tuple-element.10) | copy-start | bytes 196612
  33.1 44.0 %all-to-all-start.1 = ((f32[16,16,512]{2,1,0:T(8,128)}), f32[16,16,512]{2,1,0:T(8,128)S(1)}, u32[]{:S(2)}, u32[]{:S(2)}) async-start(f32[16,16,512]{2,1,0:T(8,128)} %broadcast_in_dim.4), calls=%async_computation.1 | async-start | bytes 1048576 | tf_op jit(solution)/shard_map/all_to_all | solution.py:31
  45.5 14.7 %collective-permute-start = (f32[16,1024]{1,0:T(8,128)S(1)}, f32[16,1024]{1,0:T(8,128)S(1)}, u32[]{:S(2)}, u32[]{:S(2)}) collective-permute-start(f32[16,1024]{1,0:T(8,128)S(1)} %copy-done.4), channel_id=1, source_target_pairs={{0,2},{2,0},{1,3},{3,1},{4,6},{6,4},{5,7},{7,5},{8,10},{10,8},{9,1... | collective-permute-start | bytes 196616 | tf_op jit(solution)/shard_map/ppermute | solution.py:35
  60.2 10.4 %collective-permute-start.1 = (f32[2,16,1024]{2,1,0:T(8,128)S(1)}, f32[2,16,1024]{2,1,0:T(8,128)S(1)}, u32[]{:S(2)}, u32[]{:S(2)}) collective-permute-start(f32[2,16,1024]{2,1,0:T(8,128)S(1)} %get-tuple-element.18.own), channel_id=1, source_target_pairs={{0,4},{4,8},{8,12},{12,16},{16,20},{20,24},{24,28},{28,0},{1,5},{5... | collective-permute-start | bytes 393224 | tf_op jit(solution)/shard_map/ppermute | solution.py:35
  65.8 6.1 %collective-permute-start.2 = (f32[2,16,1024]{2,1,0:T(8,128)S(1)}, f32[2,16,1024]{2,1,0:T(8,128)S(1)}, u32[]{:S(2)}, u32[]{:S(2)}) collective-permute-start(f32[2,16,1024]{2,1,0:T(8,128)S(1)} %get-tuple-element.18.own), channel_id=1, source_target_pairs={{0,28},{4,0},{8,4},{12,8},{16,12},{20,16},{24,20},{28,24},{1,29},{... | collective-permute-start | bytes 393224 | tf_op jit(solution)/shard_map/ppermute | solution.py:35
  72.0 12.1 %collective-permute-start.4 = (f32[2,2,16,1024]{3,2,1,0:T(8,128)S(1)}, f32[2,2,16,1024]{3,2,1,0:T(8,128)S(1)}, u32[]{:S(2)}, u32[]{:S(2)}) collective-permute-start(f32[2,2,16,1024]{3,2,1,0:T(8,128)S(1)} %get-tuple-element.15), channel_id=1, source_target_pairs={{0,24},{4,28},{8,0},{12,4},{16,8},{20,12},{24,16},{28,20},{1,25},{... | collective-permute-start | bytes 786440 | tf_op jit(solution)/shard_map/ppermute | solution.py:35
  78.0 27.9 %all-to-all-start.2 = ((f32[16,16,512]{2,1,0:T(8,128)}), f32[16,16,512]{2,1,0:T(8,128)S(1)}, u32[]{:S(2)}, u32[]{:S(2)}) async-start(f32[16,16,512]{2,1,0:T(8,128)} %broadcast_in_dim.5), calls=%async_computation.2 | async-start | bytes 1048576 | tf_op jit(solution)/shard_map/all_to_all | solution.py:31
  81.6 20.4 %collective-permute-start.3 = (f32[2,2,16,1024]{3,2,1,0:T(8,128)S(1)}, f32[2,2,16,1024]{3,2,1,0:T(8,128)S(1)}, u32[]{:S(2)}, u32[]{:S(2)}) collective-permute-start(f32[2,2,16,1024]{3,2,1,0:T(8,128)S(1)} %get-tuple-element.16), channel_id=1, source_target_pairs={{0,8},{4,12},{8,16},{12,20},{16,24},{20,28},{24,0},{28,4},{1,9},{5... | collective-permute-start | bytes 786440 | tf_op jit(solution)/shard_map/ppermute | solution.py:35
  84.1 17.9 %collective-permute-start.5 = (f32[2,16,1024]{2,1,0:T(8,128)S(1)}, f32[2,16,1024]{2,1,0:T(8,128)S(1)}, u32[]{:S(2)}, u32[]{:S(2)}) collective-permute-start(f32[2,16,1024]{2,1,0:T(8,128)S(1)} %slice_bitcast_fusion), channel_id=1, source_target_pairs={{0,28},{4,0},{8,4},{12,8},{16,12},{20,16},{24,20},{28,24},{1,29},{... | collective-permute-start | bytes 393224 | tf_op jit(solution)/shard_map/ppermute | solution.py:35
  102.1 6.1 %collective-permute-start.6 = (f32[16,16,1024]{2,1,0:T(8,128)S(1)}, f32[16,16,1024]{2,1,0:T(8,128)S(1)}, u32[]{:S(2)}, u32[]{:S(2)}) collective-permute-start(f32[16,16,1024]{2,1,0:T(8,128)S(1)} %bitcast.19), channel_id=1, source_target_pairs={{0,1},{1,0},{2,3},{3,2},{4,5},{5,4},{6,7},{7,6},{8,9},{9,8},{10,11... | collective-permute-start | bytes 3145736 | tf_op jit(solution)/shard_map/ppermute | solution.py:39
  105.9 3.8 %copy-start.1 = (f32[512]{0:T(512)S(1)}, f32[512]{0:T(512)}, u32[]{:S(2)}) copy-start(f32[512]{0:T(512)} %param.10) | copy-start | bytes 6148
  106.0 3.8 %copy-start.2 = (f32[512]{0:T(512)S(1)}, f32[512]{0:T(512)}, u32[]{:S(2)}) copy-start(f32[512]{0:T(512)} %param.11) | copy-start | bytes 6148
  106.0 3.8 %collective-permute-start.8 = (f32[256,512]{1,0:T(8,128)S(1)}, f32[256,512]{1,0:T(8,128)S(1)}, u32[]{:S(2)}, u32[]{:S(2)}) collective-permute-start(f32[256,512]{1,0:T(8,128)S(1)} %bitcast.21), channel_id=1, source_target_pairs={{0,1},{1,0},{2,3},{3,2},{4,5},{5,4},{6,7},{7,6},{8,9},{9,8},{10,11... | collective-permute-start | bytes 1572872 | tf_op jit(solution)/shard_map/ppermute | solution.py:39
Sparse Core Ops, SparseCore 0:
  10.4 81.4 all-gather.1
where the time goes:
time: 124 us; the launch traced here: 123 us
  starting transfers between devices  59.7 us (48%)
  waiting for transfers between devices  25.8 us (21%)
  between operations  13.6 us (11%)
  blocking collectives  11 us (9%)
  Pallas kernels  9.88 us (8%)
  local copies, waits for them, and re-layouts  3.36 us (3%)
    ppermute x6, starting transfers between devices, shift(): lax.ppermute(block, axis, [(i, (i + by) % size) for i in range(size)])  29.2 us
    ppermute x6, waiting for transfers between devices, shift(): lax.ppermute(block, axis, [(i, (i + by) % size) for i in range(size)])  22.7 us
    all_to_all x2, starting transfers between devices, gather(): return lax.all_to_all(copies, axis, 0, 0)  15.9 us
    ppermute x3, starting transfers between devices, swap(): return lax.ppermute(block, 'core', SWAP)  14.5 us
    all_to_all x1, blocking collectives, local(): pieces = lax.all_to_all(mine.reshape(16, 16, SIZE_K), OUTER, 0, 0)  11 us
    pallas_call x1, Pallas kernels, product(): pl.pallas_call(product_kernel, out_shape=jax.ShapeDtypeStruct((512, 768),...  5.5 us
    ppermute x3, waiting for transfers between devices, swap(): return lax.ppermute(block, 'core', SWAP)  3.08 us
  transfers between devices with their start and end apart: 12, of which 8 were waited for; matrix products, arithmetic and copies ran while one was open for 2% of the time, Pallas kernels for 2%

commit v1 on v0

--- a/solution.py
+++ b/solution.py
@@ -11,7 +11,6 @@
 ALL = ROW + COL
 Z = ("zh", "zl")
 OUTER = ("x", "zl", "yl")
-INNER = ("yh", "zh")
 SIZES = (4, 4, 4, 2, 2, 2)
 SIZE_K = 512
 HALF = 256
@@ -143,8 +142,8 @@
     )(core_index.reshape(1), own, got, singular.reshape(1, -1))
 
 
-def place_kernel(z, below, own, above, mid_below, mid_above, last_above, out):
-    blocks = [own[...], above[...], mid_above[0], mid_above[1], last_above[...]]
+def place_kernel(z, below, own, mid_below, mid_above, last_above, out):
+    blocks = [own[...], mid_above[0], mid_above[1], last_above[0], last_above[1]]
     blocks = blocks + [mid_below[0], mid_below[1], below[...]]
     for i, block in enumerate(blocks):
         out[lax.rem(z[0] + i, 8)] = block
@@ -249,13 +248,13 @@
     pieces = lax.all_to_all(mine.reshape(16, 16, SIZE_K), OUTER, 0, 0)
 
     own = jnp.stack([jnp.where(at_low, left_pair, other), jnp.where(at_low, other, left_pair)])
-    below, above = shift(own, Z, 8, 1), shift(own, Z, 8, -1)
-
-    mid_below = shift(jnp.stack([below, own]), Z, 8, 2)
-    mid_above = shift(jnp.stack([own, above]), Z, 8, -2)
-    pieces = gather(jnp.sum(pieces, axis=0), INNER, 16)
-    last_above = shift(mid_above[1], Z, 8, -1)
-    blocks = (below, own, above, mid_below, mid_above, last_above)
+    below = shift(own, Z, 8, 1)
+    pair = jnp.stack([below, own])
+    mid_below, mid_above = shift(pair, Z, 8, 2), shift(pair, Z, 8, -2)
+    pieces = gather(jnp.sum(pieces, axis=0), "yh", 4)
+    pieces = gather(jnp.sum(pieces, axis=0), "zh", 4)
+    last_above = shift(mid_above, Z, 8, -2)
+    blocks = (below, own, mid_below, mid_above, last_above)
     line = assemble(place_kernel, (8, 2, 16, 1024), lax.axis_index(Z), *blocks)
     line = line.reshape(16, 16, 1024)
     rows = jnp.sum(pieces, axis=0)

time: 124 us -> 116 us (0.935)
  blocking collectives: 11 us -> 0 us
  starting transfers between devices: 59.7 us -> 64.1 us
  waiting for transfers between devices: 25.8 us -> 22.1 us
    all_to_all x1 -> x0, blocking collectives: 11 us -> none  [local(): pieces = lax.all_to_all(mine.reshape(16, 16, SIZE_K), OUTER, 0, 0)]
    ppermute x6 -> x5, waiting for transfers between devices: 22.7 us -> 12.7 us  [shift(): lax.ppermute(block, axis, [(i, (i + by) % size) for i in range(size)])]
    ppermute x6 -> x5, starting transfers between devices: 29.2 us -> 19.6 us  [shift(): lax.ppermute(block, axis, [(i, (i + by) % size) for i in range(size)])]
    ppermute x3, starting transfers between devices: 14.5 us -> 20.8 us  [swap(): return lax.ppermute(block, 'core', SWAP)]
    all_to_all x2 -> x3, waiting for transfers between devices: 0.01 us -> 6.24 us  [gather(): return lax.all_to_all(copies, axis, 0, 0)]
    all_to_all x2 -> x3, starting transfers between devices: 15.9 us -> 20.2 us  [gather(): return lax.all_to_all(copies, axis, 0, 0)]
    all_to_all x0 -> x1, starting transfers between devices: none -> 3.57 us  [local(): pieces = lax.all_to_all(mine.reshape(16, 16, SIZE_K), OUTER, 0, 0)]
  transfers between devices with their start and end apart: 12 -> 13, of which waited for: 8 -> 7; matrix products, arithmetic and copies ran while one was open for 2% -> 2% of each run, Pallas kernels for 2% -> 3%
where the time goes in v1:
time: 116 us; the launch traced here: 114 us
  starting transfers between devices  64.1 us (55%)
  waiting for transfers between devices  22.1 us (19%)
  between operations  13.6 us (12%)
  Pallas kernels  10.7 us (9%)
  local copies, waits for them, and re-layouts  3.83 us (3%)
    ppermute x3, starting transfers between devices, swap(): return lax.ppermute(block, 'core', SWAP)  20.8 us
    all_to_all x3, starting transfers between devices, gather(): return lax.all_to_all(copies, axis, 0, 0)  20.2 us
    ppermute x5, starting transfers between devices, shift(): lax.ppermute(block, axis, [(i, (i + by) % size) for i in range(size)])  19.6 us
    ppermute x5, waiting for transfers between devices, shift(): lax.ppermute(block, axis, [(i, (i + by) % size) for i in range(size)])  12.7 us
    all_to_all x3, waiting for transfers between devices, gather(): return lax.all_to_all(copies, axis, 0, 0)  6.24 us
    pallas_call x1, Pallas kernels, product(): pl.pallas_call(product_kernel, out_shape=jax.ShapeDtypeStruct((512, 768),...  5.5 us
    all_to_all x1, starting transfers between devices, local(): pieces = lax.all_to_all(mine.reshape(16, 16, SIZE_K), OUTER, 0, 0)  3.57 us
    ppermute x3, waiting for transfers between devices, swap(): return lax.ppermute(block, 'core', SWAP)  3.08 us
  transfers between devices with their start and end apart: 13, of which 7 were waited for; matrix products, arithmetic and copies ran while one was open for 2% of the time, Pallas kernels for 3%

profile of v1, /device:TPU:1, one launch (start us, length us, event | category | flops | bytes accessed | tf_op | source)
XLA Modules:
  0.0 114.4 jit_solution(3025273502075287661)
XLA Ops:
  6.5 1.8 %pack.1 = (f32[48,1024]{1,0:T(8,128)}, f32[16,1024]{1,0:T(8,128)}, f32[64,1024]{1,0:T(8,128)}) custom-call(f32[16,512]{1,0:T(8,128)} %left.1, f32[16,512]{1,0:T(8,128)} %left_cot.1, f32[48,512]{1,0:T(8,128)} %right.1, f32[48,512]{1,0:T(8,128)} %right_cot.1), custom_call_target="tpu_custom_call" | custom-call | bytes 1048576 | tf_op jit(solution)/shard_map/pack/pallas_call | solution.py:70
  8.3 0.0 all-gather.2.cloned.1.call-update
  8.3 8.7 %collective-permute-start.6 = (f32[64,1024]{1,0:T(8,128)}, f32[64,1024]{1,0:T(8,128)S(1)}, u32[]{:S(2)}, u32[]{:S(2)}) collective-permute-start(f32[64,1024]{1,0:T(8,128)} %get-tuple-element.11.own), channel_id=1, source_target_pairs={{0,1},{1,0},{2,3},{3,2},{4,5},{5,4},{6,7},{7,6},{8,9},{9,8},{10,11... | collective-permute-start | bytes 786440 | tf_op jit(solution)/shard_map/ppermute | solution.py:38
  17.1 1.3 %collective-permute-done.6.got = f32[64,1024]{1,0:T(8,128)S(1)} collective-permute-done((f32[64,1024]{1,0:T(8,128)}, f32[64,1024]{1,0:T(8,128)S(1)}, u32[]{:S(2)}, u32[]{:S(2)}) %collective-permute-start.6) | collective-permute-done | bytes 262176 | tf_op jit(solution)/shard_map/ppermute | solution.py:38
  18.5 0.7 copy-done
  19.1 0.9 copy-done.3
  20.1 1.9 %half_core.1 = f32[256,512]{1,0:T(8,128)} custom-call(s32[1]{0:T(128)} %bitcast.index.core_index, f32[64,1024]{1,0:T(8,128)S(1)} %copy-done.3, f32[64,1024]{1,0:T(8,128)S(1)} %collective-permute-done.6.got, f32[1,512]{1,0:T(1,128)S(1)} %bitcast.21), custom_call_target="tpu_custom_call" | custom-call | flops 603979776 | bytes 1048576 | tf_op jit(solution)/shard_map/half_core/pallas_call | solution.py:126
  22.0 3.6 %all-to-all-start = ((f32[16,16,512]{2,1,0:T(8,128)}), f32[16,16,512]{2,1,0:T(8,128)S(1)}, u32[]{:S(2)}, u32[]{:S(2)}) async-start(f32[16,16,512]{2,1,0:T(8,128)} %bitcast.9), calls=%async_computation | async-start | bytes 1048576 | tf_op jit(solution)/shard_map/all_to_all | solution.py:248
  25.6 3.1 %collective-permute-start = (f32[16,1024]{1,0:T(8,128)S(1)}, f32[16,1024]{1,0:T(8,128)S(1)}, u32[]{:S(2)}, u32[]{:S(2)}) collective-permute-start(f32[16,1024]{1,0:T(8,128)S(1)} %copy-done.4), channel_id=1, source_target_pairs={{0,2},{2,0},{1,3},{3,1},{4,6},{6,4},{5,7},{7,5},{8,10},{10,8},{9,1... | collective-permute-start | bytes 196616 | tf_op jit(solution)/shard_map/ppermute | solution.py:34
  28.8 5.8 %collective-permute-done = f32[16,1024]{1,0:T(8,128)S(1)} collective-permute-done((f32[16,1024]{1,0:T(8,128)S(1)}, f32[16,1024]{1,0:T(8,128)S(1)}, u32[]{:S(2)}, u32[]{:S(2)}) %collective-permute-start) | collective-permute-done | bytes 65568 | tf_op jit(solution)/shard_map/ppermute | solution.py:34
  34.7 0.7 broadcast_in_dim.6
  35.3 3.7 %all-to-all-start.1 = ((f32[4,16,512]{2,1,0:T(8,128)}), f32[4,16,512]{2,1,0:T(8,128)S(1)}, u32[]{:S(2)}, u32[]{:S(2)}) async-start(f32[4,16,512]{2,1,0:T(8,128)} %broadcast_in_dim.6), calls=%async_computation.1 | async-start | bytes 262144 | tf_op jit(solution)/shard_map/all_to_all | solution.py:30
  39.0 3.6 %collective-permute-start.1 = (f32[2,16,1024]{2,1,0:T(8,128)S(1)}, f32[2,16,1024]{2,1,0:T(8,128)S(1)}, u32[]{:S(2)}, u32[]{:S(2)}) collective-permute-start(f32[2,16,1024]{2,1,0:T(8,128)S(1)} %get-tuple-element.16.own), channel_id=1, source_target_pairs={{0,4},{4,8},{8,12},{12,16},{16,20},{20,24},{24,28},{28,0},{1,5},{5... | collective-permute-start | bytes 393224 | tf_op jit(solution)/shard_map/ppermute | solution.py:34
  42.6 4.4 %all-to-all-done.1 = f32[4,16,512]{2,1,0:T(8,128)S(1)} async-done(((f32[4,16,512]{2,1,0:T(8,128)}), f32[4,16,512]{2,1,0:T(8,128)S(1)}, u32[]{:S(2)}, u32[]{:S(2)}) %all-to-all-start.1) | async-done | bytes 131104 | tf_op jit(solution)/shard_map/all_to_all | solution.py:30
  47.0 0.7 broadcast_in_dim.7
  47.7 10.9 %all-to-all-start.2 = ((f32[4,16,512]{2,1,0:T(8,128)}), f32[4,16,512]{2,1,0:T(8,128)S(1)}, u32[]{:S(2)}, u32[]{:S(2)}) async-start(f32[4,16,512]{2,1,0:T(8,128)} %broadcast_in_dim.7), calls=%async_computation.2 | async-start | bytes 262144 | tf_op jit(solution)/shard_map/all_to_all | solution.py:30
  58.5 5.5 %collective-permute-start.3 = (f32[2,2,16,1024]{3,2,1,0:T(8,128)S(1)}, f32[2,2,16,1024]{3,2,1,0:T(8,128)S(1)}, u32[]{:S(2)}, u32[]{:S(2)}) collective-permute-start(f32[2,2,16,1024]{3,2,1,0:T(8,128)S(1)} %pad_maximum_fusion), channel_id=1, source_target_pairs={{0,24},{4,28},{8,0},{12,4},{16,8},{20,12},{24,16},{28,20},{1,25},{... | collective-permute-start | bytes 786440 | tf_op jit(solution)/shard_map/ppermute | solution.py:34
  64.0 1.8 %all-to-all-done.2 = f32[4,16,512]{2,1,0:T(8,128)S(1)} async-done(((f32[4,16,512]{2,1,0:T(8,128)}), f32[4,16,512]{2,1,0:T(8,128)S(1)}, u32[]{:S(2)}, u32[]{:S(2)}) %all-to-all-start.2) | async-done | bytes 131104 | tf_op jit(solution)/shard_map/all_to_all | solution.py:30
  65.9 0.9 broadcast_in_dim.8
  66.7 5.7 %all-to-all-start.3 = ((f32[16,16,512]{2,1,0:T(8,128)}), f32[16,16,512]{2,1,0:T(8,128)S(1)}, u32[]{:S(2)}, u32[]{:S(2)}) async-start(f32[16,16,512]{2,1,0:T(8,128)} %broadcast_in_dim.8), calls=%async_computation.3 | async-start | bytes 1048576 | tf_op jit(solution)/shard_map/all_to_all | solution.py:30
  72.4 2.5 %collective-permute-start.2 = (f32[2,2,16,1024]{3,2,1,0:T(8,128)S(1)}, f32[2,2,16,1024]{3,2,1,0:T(8,128)S(1)}, u32[]{:S(2)}, u32[]{:S(2)}) collective-permute-start(f32[2,2,16,1024]{3,2,1,0:T(8,128)S(1)} %pad_maximum_fusion), channel_id=1, source_target_pairs={{0,8},{4,12},{8,16},{12,20},{16,24},{20,28},{24,0},{28,4},{1,9},{5... | collective-permute-start | bytes 786440 | tf_op jit(solution)/shard_map/ppermute | solution.py:34
  74.9 4.9 %collective-permute-start.4 = (f32[2,2,16,1024]{3,2,1,0:T(8,128)S(1)}, f32[2,2,16,1024]{3,2,1,0:T(8,128)S(1)}, u32[]{:S(2)}, u32[]{:S(2)}) collective-permute-start(f32[2,2,16,1024]{3,2,1,0:T(8,128)S(1)} %collective-permute-done.3.mid_above), channel_id=1, source_target_pairs={{0,24},{4,28},{8,0},{12,4},{16,8},{20,12},{24,16},{28,20},{1,25},{... | collective-permute-start | bytes 786440 | tf_op jit(solution)/shard_map/ppermute | solution.py:34
  79.8 6.9 %collective-permute-done.2.mid_below = f32[2,2,16,1024]{3,2,1,0:T(8,128)S(1)} collective-permute-done((f32[2,2,16,1024]{3,2,1,0:T(8,128)S(1)}, f32[2,2,16,1024]{3,2,1,0:T(8,128)S(1)}, u32[]{:S(2)}, u32[]{:S(2)}) %collective-permute-start.2) | collective-permute-done | bytes 262176 | tf_op jit(solution)/shard_map/ppermute | solution.py:34
  86.7 0.1 shard_map.64
  86.8 10.1 %collective-permute-start.5 = (f32[16,16,1024]{2,1,0:T(8,128)S(1)}, f32[16,16,1024]{2,1,0:T(8,128)S(1)}, u32[]{:S(2)}, u32[]{:S(2)}) collective-permute-start(f32[16,16,1024]{2,1,0:T(8,128)S(1)} %bitcast.16), channel_id=1, source_target_pairs={{0,1},{1,0},{2,3},{3,2},{4,5},{5,4},{6,7},{7,6},{8,9},{9,8},{10,11... | collective-permute-start | bytes 3145736 | tf_op jit(solution)/shard_map/ppermute | solution.py:38
  96.9 1.9 %collective-permute-start.7 = (f32[256,512]{1,0:T(8,128)S(1)}, f32[256,512]{1,0:T(8,128)S(1)}, u32[]{:S(2)}, u32[]{:S(2)}) collective-permute-start(f32[256,512]{1,0:T(8,128)S(1)} %bitcast.18), channel_id=1, source_target_pairs={{0,1},{1,0},{2,3},{3,2},{4,5},{5,4},{6,7},{7,6},{8,9},{9,8},{10,11... | collective-permute-start | bytes 1572872 | tf_op jit(solution)/shard_map/ppermute | solution.py:38
  98.9 0.3 collective-permute-done.5.theirs
  99.2 0.1 shard_map.65
  99.3 1.4 %collective-permute-done.7.other_half = f32[256,512]{1,0:T(8,128)S(1)} collective-permute-done((f32[256,512]{1,0:T(8,128)S(1)}, f32[256,512]{1,0:T(8,128)S(1)}, u32[]{:S(2)}, u32[]{:S(2)}) %collective-permute-start.7) | collective-permute-done | bytes 524320 | tf_op jit(solution)/shard_map/ppermute | solution.py:38
  100.7 1.3 %panel.1 = (bf16[512,1024]{1,0:T(8,128)(2,1)S(1)}, bf16[512,1024]{1,0:T(8,128)(2,1)S(1)}) custom-call(s32[1]{0:T(128)} %bitcast.index.core_index, f32[512,1024]{1,0:T(8,128)S(1)} %bitcast.15, f32[256,512]{1,0:T(8,128)S(1)} %bitcast.19, f32[256,512]{1,0:T(8,128)S(1)} %collective-permute-done.7.other_half, f32[1,512]{1,0:T(1,128)S(1)} %bitcast.22, ...), custom_call_target="tpu_custom_call" | custom-call | flops 805306368 | bytes 5242880 | tf_op jit(solution)/shard_map/panel/pallas_call | solution.py:196
  102.0 0.0 all-gather.2.cloned.1.call-done.rights
  102.0 5.5 %product.1 = f32[512,768]{1,0:T(8,128)} custom-call(bf16[512,1024]{1,0:T(8,128)(2,1)S(1)} %get-tuple-element.12.high, bf16[512,1024]{1,0:T(8,128)(2,1)S(1)} %get-tuple-element.13.low, f32[768,1024]{1,0:T(8,128)} %all-gather.2.cloned.1.call-done.rights), custom_call_target="tpu_custom_call" | custom-call | flops 2415919104 | bytes 7340032 | tf_op jit(solution)/shard_map/product/pallas_call | solution.py:225
  (20 shorter events, 0.1 us)
Async XLA Ops:
  6.5 95.5 %all-gather.2.cloned.1.call-start = ((), (), s32[]{:S(2)}) async-start(), calls=%async_computation.4 | async-start | bytes 3342336 | tf_op jit(solution)/shard_map/all_gather | solution.py:244
  8.3 17.3 %copy-start.4 = (f32[16,1024]{1,0:T(8,128)S(1)}, f32[16,1024]{1,0:T(8,128)}, u32[]{:S(2)}) copy-start(f32[16,1024]{1,0:T(8,128)} %get-tuple-element.10) | copy-start | bytes 196612
  8.3 10.1 %collective-permute-start.6 = (f32[64,1024]{1,0:T(8,128)}, f32[64,1024]{1,0:T(8,128)S(1)}, u32[]{:S(2)}, u32[]{:S(2)}) collective-permute-start(f32[64,1024]{1,0:T(8,128)} %get-tuple-element.11.own), channel_id=1, source_target_pairs={{0,1},{1,0},{2,3},{3,2},{4,5},{5,4},{6,7},{7,6},{8,9},{9,8},{10,11... | collective-permute-start | bytes 786440 | tf_op jit(solution)/shard_map/ppermute | solution.py:38
  18.5 0.7 copy-start
  19.1 0.9 copy-start.3
  22.0 12.6 %all-to-all-start = ((f32[16,16,512]{2,1,0:T(8,128)}), f32[16,16,512]{2,1,0:T(8,128)S(1)}, u32[]{:S(2)}, u32[]{:S(2)}) async-start(f32[16,16,512]{2,1,0:T(8,128)} %bitcast.9), calls=%async_computation | async-start | bytes 1048576 | tf_op jit(solution)/shard_map/all_to_all | solution.py:248
  25.6 9.0 %collective-permute-start = (f32[16,1024]{1,0:T(8,128)S(1)}, f32[16,1024]{1,0:T(8,128)S(1)}, u32[]{:S(2)}, u32[]{:S(2)}) collective-permute-start(f32[16,1024]{1,0:T(8,128)S(1)} %copy-done.4), channel_id=1, source_target_pairs={{0,2},{2,0},{1,3},{3,1},{4,6},{6,4},{5,7},{7,5},{8,10},{10,8},{9,1... | collective-permute-start | bytes 196616 | tf_op jit(solution)/shard_map/ppermute | solution.py:34
  35.3 11.7 %all-to-all-start.1 = ((f32[4,16,512]{2,1,0:T(8,128)}), f32[4,16,512]{2,1,0:T(8,128)S(1)}, u32[]{:S(2)}, u32[]{:S(2)}) async-start(f32[4,16,512]{2,1,0:T(8,128)} %broadcast_in_dim.6), calls=%async_computation.1 | async-start | bytes 262144 | tf_op jit(solution)/shard_map/all_to_all | solution.py:30
  39.0 19.5 %collective-permute-start.1 = (f32[2,16,1024]{2,1,0:T(8,128)S(1)}, f32[2,16,1024]{2,1,0:T(8,128)S(1)}, u32[]{:S(2)}, u32[]{:S(2)}) collective-permute-start(f32[2,16,1024]{2,1,0:T(8,128)S(1)} %get-tuple-element.16.own), channel_id=1, source_target_pairs={{0,4},{4,8},{8,12},{12,16},{16,20},{20,24},{24,28},{28,0},{1,5},{5... | collective-permute-start | bytes 393224 | tf_op jit(solution)/shard_map/ppermute | solution.py:34
  47.7 18.2 %all-to-all-start.2 = ((f32[4,16,512]{2,1,0:T(8,128)}), f32[4,16,512]{2,1,0:T(8,128)S(1)}, u32[]{:S(2)}, u32[]{:S(2)}) async-start(f32[4,16,512]{2,1,0:T(8,128)} %broadcast_in_dim.7), calls=%async_computation.2 | async-start | bytes 262144 | tf_op jit(solution)/shard_map/all_to_all | solution.py:30
  58.5 16.3 %collective-permute-start.3 = (f32[2,2,16,1024]{3,2,1,0:T(8,128)S(1)}, f32[2,2,16,1024]{3,2,1,0:T(8,128)S(1)}, u32[]{:S(2)}, u32[]{:S(2)}) collective-permute-start(f32[2,2,16,1024]{3,2,1,0:T(8,128)S(1)} %pad_maximum_fusion), channel_id=1, source_target_pairs={{0,24},{4,28},{8,0},{12,4},{16,8},{20,12},{24,16},{28,20},{1,25},{... | collective-permute-start | bytes 786440 | tf_op jit(solution)/shard_map/ppermute | solution.py:34
  66.7 30.2 %all-to-all-start.3 = ((f32[16,16,512]{2,1,0:T(8,128)}), f32[16,16,512]{2,1,0:T(8,128)S(1)}, u32[]{:S(2)}, u32[]{:S(2)}) async-start(f32[16,16,512]{2,1,0:T(8,128)} %broadcast_in_dim.8), calls=%async_computation.3 | async-start | bytes 1048576 | tf_op jit(solution)/shard_map/all_to_all | solution.py:30
  72.4 14.3 %collective-permute-start.2 = (f32[2,2,16,1024]{3,2,1,0:T(8,128)S(1)}, f32[2,2,16,1024]{3,2,1,0:T(8,128)S(1)}, u32[]{:S(2)}, u32[]{:S(2)}) collective-permute-start(f32[2,2,16,1024]{3,2,1,0:T(8,128)S(1)} %pad_maximum_fusion), channel_id=1, source_target_pairs={{0,8},{4,12},{8,16},{12,20},{16,24},{20,28},{24,0},{28,4},{1,9},{5... | collective-permute-start | bytes 786440 | tf_op jit(solution)/shard_map/ppermute | solution.py:34
  74.9 11.8 %collective-permute-start.4 = (f32[2,2,16,1024]{3,2,1,0:T(8,128)S(1)}, f32[2,2,16,1024]{3,2,1,0:T(8,128)S(1)}, u32[]{:S(2)}, u32[]{:S(2)}) collective-permute-start(f32[2,2,16,1024]{3,2,1,0:T(8,128)S(1)} %collective-permute-done.3.mid_above), channel_id=1, source_target_pairs={{0,24},{4,28},{8,0},{12,4},{16,8},{20,12},{24,16},{28,20},{1,25},{... | collective-permute-start | bytes 786440 | tf_op jit(solution)/shard_map/ppermute | solution.py:34
  86.8 12.4 %collective-permute-start.5 = (f32[16,16,1024]{2,1,0:T(8,128)S(1)}, f32[16,16,1024]{2,1,0:T(8,128)S(1)}, u32[]{:S(2)}, u32[]{:S(2)}) collective-permute-start(f32[16,16,1024]{2,1,0:T(8,128)S(1)} %bitcast.16), channel_id=1, source_target_pairs={{0,1},{1,0},{2,3},{3,2},{4,5},{5,4},{6,7},{7,6},{8,9},{9,8},{10,11... | collective-permute-start | bytes 3145736 | tf_op jit(solution)/shard_map/ppermute | solution.py:38
  96.9 3.8 %copy-start.1 = (f32[512]{0:T(512)S(1)}, f32[512]{0:T(512)}, u32[]{:S(2)}) copy-start(f32[512]{0:T(512)} %param.10) | copy-start | bytes 6148
  96.9 3.8 %copy-start.2 = (f32[512]{0:T(512)S(1)}, f32[512]{0:T(512)}, u32[]{:S(2)}) copy-start(f32[512]{0:T(512)} %param.11) | copy-start | bytes 6148
  96.9 3.8 %collective-permute-start.7 = (f32[256,512]{1,0:T(8,128)S(1)}, f32[256,512]{1,0:T(8,128)S(1)}, u32[]{:S(2)}, u32[]{:S(2)}) collective-permute-start(f32[256,512]{1,0:T(8,128)S(1)} %bitcast.18), channel_id=1, source_target_pairs={{0,1},{1,0},{2,3},{3,2},{4,5},{5,4},{6,7},{7,6},{8,9},{9,8},{10,11... | collective-permute-start | bytes 1572872 | tf_op jit(solution)/shard_map/ppermute | solution.py:38
Sparse Core Ops, SparseCore 0:
  10.4 84.9 all-gather.1
